TPU v7x, 32 devices: a whole 2x2x4 slice. The times are simulated.
32 devices in a mesh: comp: 8 (over y, x, core), strip: 4 (over z).
Axes of the slice: x: 2, y: 2, z: 4, core: 2. Of those that a mesh axis runs over, the one named last changes fastest.
Arguments:
- energy: bfloat16 [1152, 64, 512], P('comp', 'strip'), may hold values from 0.049804688 to 2
- heading: float32 [1152], P('comp'), may hold values from -3.140625 to 3.140625
- growth: float32 [1152], P('comp'), may hold values from 0.005 to 0.05
- courant: float32 [1152, 2], P('comp'), may hold values from -0.45 to 0.45
- dissip: float32 [1152], replicated, may hold values from 0.05 to 0.5
- mixing: bfloat16 [1152, 1152], replicated, may hold values from -0.1875 to 0.1875
- transfer: bfloat16 [1152, 1152], replicated, may hold values from -0.046875 to 0.046875
- pattern: int32 [1152], replicated, may hold values from 0 to 1151, each once
- regime_winds: float32 [8, 2], replicated, may hold values from -8 to 8
- regime: int32 [32, 32], P('strip'), may hold values from 0 to 7
- seeds: int32 [32, 32], P('strip'), may hold values from 0 to 1023
- sea_mask: int32 [64, 512], P('strip'), may hold values 0 or 1
Outputs:
- energy_out: float32 [1152, 64, 512], P('comp', 'strip')
Inputs may be any that keep to these rules, and one draw needn't show every extreme that they name: `pattern`: each component is named exactly once.
All inputs are finite; a program needn't handle non-finite values. No bound on the sum of `sea_mask` on one device may be relied on, other than what follows from the above.
Results may differ from a plain program's by a relative error of at most 0.0008.
Values may be sent and summed in bfloat16 or wider, within the bound.
No kernel may reach another device: no remote copies, remote signals or barrier semaphores. Data moves between devices by JAX's collectives and lax.ppermute only.
A program may use at most 192 MiB of HBM per device.

v0:
```python
import jax
import jax.numpy as jnp
from jax import lax
from jax.sharding import PartitionSpec as P

SUBSTEPS = 4
TILE_ROWS = 2
TILE_COLS = 16


def with_halo(block, sides, width):
    for axis, dim in sides:
        count = lax.axis_size(axis)
        forward = [(i, i + 1) for i in range(count - 1)]
        backward = [(target, source) for source, target in forward]
        low = lax.ppermute(
            lax.slice_in_dim(block, block.shape[dim] - width, None, axis=dim), axis, forward
        )
        high = lax.ppermute(lax.slice_in_dim(block, 0, width, axis=dim), axis, backward)
        block = jnp.concatenate([low, block, high], axis=dim)
    return block


def strip_winds(regime_winds, regime, seeds):
    levels = jnp.arange(regime_winds.shape[0], dtype=jnp.int32)
    onehot = (regime[..., None] == levels).astype(jnp.float32)
    base_u = jnp.sum(onehot * regime_winds[:, 0], axis=-1)
    base_v = jnp.sum(onehot * regime_winds[:, 1], axis=-1)
    tile_u = base_u + 0.25 * (seeds % 13 - 6).astype(jnp.float32)
    tile_v = base_v + 0.4 * (seeds % 7 - 3).astype(jnp.float32)
    wind_u = jnp.repeat(jnp.repeat(tile_u, TILE_ROWS, axis=0), TILE_COLS, axis=1)
    wind_v = jnp.repeat(jnp.repeat(tile_v, TILE_ROWS, axis=0), TILE_COLS, axis=1)
    return (wind_u, wind_v)


def cell_terms(spectra, mixing, transfer, pattern, dissip):
    spectrum_shape = spectra.shape
    flattened = spectra.reshape(spectrum_shape[0], -1)
    mixed_terms = jnp.dot(mixing, flattened, preferred_element_type=jnp.float32)
    partner = jnp.take(flattened, pattern, axis=0)
    product = (mixed_terms * partner.astype(jnp.float32)).astype(jnp.bfloat16)
    nonlinear = jnp.dot(transfer, product, preferred_element_type=jnp.float32)
    widened = flattened.astype(jnp.float32)
    mean_energy = jnp.sum(widened, axis=0) / spectrum_shape[0]
    result = nonlinear - dissip[:, None] * mean_energy[None, :] * widened
    return result.astype(jnp.bfloat16).reshape(spectrum_shape)


def advect(padded, sea_field, courant_x, courant_y):
    flux_y = (
        jnp.maximum(courant_y, 0.0) * padded[..., :-1, :]
        + jnp.minimum(courant_y, 0.0) * padded[..., 1:, :]
    )
    center = padded[..., 1:-1, :]
    widths = [(0, 0)] * (center.ndim - 1) + [(1, 1)]
    padded_x = jnp.pad(center, widths)
    flux_x = (
        jnp.maximum(courant_x, 0.0) * padded_x[..., :-1]
        + jnp.minimum(courant_x, 0.0) * padded_x[..., 1:]
    )
    return (
        center - (flux_x[..., 1:] - flux_x[..., :-1]) - (flux_y[..., 1:, :] - flux_y[..., :-1, :])
    ) * sea_field


def per_device(
    energy,
    heading,
    growth,
    courant,
    dissip,
    mixing,
    transfer,
    pattern,
    regime_winds,
    regime,
    seeds,
    sea_mask,
):
    wind_u, wind_v = strip_winds(regime_winds, regime, seeds)
    widened = energy.astype(jnp.float32)
    drive = (
        wind_u[None] * jnp.cos(heading)[:, None, None]
        + wind_v[None] * jnp.sin(heading)[:, None, None]
    )
    input_term = growth[:, None, None] * jnp.maximum(0.0, drive) * widened
    returned = lax.all_to_all(
        cell_terms(
            lax.all_to_all(energy, "comp", split_axis=1, concat_axis=0, tiled=True),
            mixing,
            transfer,
            pattern,
            dissip,
        ),
        "comp",
        split_axis=0,
        concat_axis=1,
        tiled=True,
    )
    energy_field = widened + input_term + returned.astype(jnp.float32)
    sea_field = sea_mask.astype(jnp.float32)
    courant_x = courant[:, 0][:, None, None]
    courant_y = courant[:, 1][:, None, None]
    for substep in range(SUBSTEPS):
        padded = with_halo(energy_field, (("strip", 1),), 1)
        energy_field = advect(padded, sea_field, courant_x, courant_y)
    return energy_field


def solution(mesh):
    placed = (
        P("comp", "strip", None),
        P("comp"),
        P("comp"),
        P("comp", None),
        P(),
        P(),
        P(),
        P(),
        P(),
        P("strip", None),
        P("strip", None),
        P("strip", None),
    )
    return jax.shard_map(
        per_device, mesh=mesh, in_specs=placed, out_specs=P("comp", "strip", None), check_vma=False
    )
```

profile of v0, /device:TPU:26, one launch (start us, length us, event | category | flops | bytes accessed | tf_op | source)
XLA Modules:
  0.0 194.6 jit_solution(15152616332735893977)
XLA Ops:
  0.0 4.5 %copy.33 = bf16[144,16,512]{2,0,1:T(8,128)(2,1)} copy(bf16[144,16,512]{2,1,0:T(8,128)(2,1)} %param.12) | data formatting | bytes 4718592 | tf_op args[0]
  4.5 4.8 %all-to-all-start = ((bf16[144,16,512]{2,0,1:T(8,128)(2,1)}), bf16[144,16,512]{2,0,1:T(8,128)(2,1)}, u32[]{:S(2)}, u32[]{:S(2)}) async-start(bf16[144,16,512]{2,0,1:T(8,128)(2,1)} %copy.33), calls=%async_computation | async-start | bytes 4718592 | tf_op jit(solution)/shard_map/all_to_all | solution.py:89
  9.4 28.0 %all-to-all-done = bf16[144,16,512]{2,0,1:T(8,128)(2,1)} async-done(((bf16[144,16,512]{2,0,1:T(8,128)(2,1)}), bf16[144,16,512]{2,0,1:T(8,128)(2,1)}, u32[]{:S(2)}, u32[]{:S(2)}) %all-to-all-start) | async-done | bytes 2359328 | tf_op jit(solution)/shard_map/all_to_all | solution.py:89
  37.4 4.2 %convert_reduce_fusion = f32[2,512]{1,0:T(2,128)S(1)} fusion(bf16[144,8,2,512]{3,0,2,1:T(8,128)(2,1)} %bitcast.4), kind=kLoop, calls=%fused_computation.59 | loop fusion | flops 2358272 | bytes 2363392 | tf_op jit(solution)/shard_map/reduce_sum | solution.py:44
  41.6 4.1 %copy.35 = bf16[144,8,2,512]{3,2,0,1:T(2,128)(2,1)S(1)} copy(bf16[144,8,2,512]{3,0,2,1:T(8,128)(2,1)} %bitcast.4) | data formatting | bytes 4718592 | tf_op jit(solution)/shard_map/all_to_all | solution.py:89
  45.7 2.0 %copy.41 = bf16[144,8,2,512]{3,1,2,0:T(8,128)(2,1)} copy(bf16[144,8,2,512]{3,2,1,0:T(2,128)(2,1)S(1)} %bitcast.37) | data formatting | bytes 4718592
  47.7 4.4 %copy.36 = bf16[1152,1024]{0,1:T(8,128)(2,1)} copy(bf16[1152,1024]{1,0:T(8,128)(2,1)} %bitcast.33) | data formatting | bytes 4718592 | tf_op jit(solution)/shard_map/reshape | solution.py:38
  52.1 8.6 %gather_fusion = bf16[1152,1024]{1,0:T(8,128)(2,1)} fusion(bf16[1152,1024]{1,0:T(8,128)(2,1)} %bitcast.34, s32[2048]{0:T(1024)S(1)} %pad_clamp_fusion), kind=kCustom, calls=%fused_computation | custom fusion | bytes 4723200 | tf_op jit(solution)/shard_map/jit(_take)/gather | solution.py:40
  60.7 12.2 %fusion.29 = bf16[1152,1024]{0,1:T(8,128)(2,1)} fusion(bf16[1152,1024]{0,1:T(8,128)(2,1)} %copy.36, bf16[1152,1152]{1,0:T(8,128)(2,1)S(1)} %copy-done, f32[1024]{0:T(1024)S(1)} %bitcast.57, f32[1152]{0:T(1024)S(1)} %copy-done.11, bf16[1152,1152]{1,0:T(8,128)(2,1)} %param.17, bf16[1152,1024]{1,0:T(8,128)(2,1)} %bitcast.35, ...), kind=kOutput, calls=%fused_computation.58 | convolution fusion | flops 5446434816 | bytes 14755456 | tf_op jit(solution)/shard_map/dot_general | solution.py:42
  72.9 6.8 %copy.37 = bf16[1152,2,512]{2,1,0:T(2,128)(2,1)} copy(bf16[1152,2,512]{0,2,1:T(8,128)(2,1)} %bitcast.38) | data formatting | bytes 4718592 | tf_op jit(solution)/shard_map/reshape | solution.py:46
  79.7 5.8 %all-to-all-start.1 = ((bf16[1152,2,512]{2,1,0:T(2,128)(2,1)}), bf16[1152,2,512]{2,1,0:T(2,128)(2,1)}, u32[]{:S(2)}, u32[]{:S(2)}) async-start(bf16[1152,2,512]{2,1,0:T(2,128)(2,1)} %copy.37), calls=%async_computation.1 | async-start | bytes 4718592 | tf_op jit(solution)/shard_map/all_to_all | solution.py:87
  86.3 27.2 %all-to-all-done.1 = bf16[1152,2,512]{2,1,0:T(2,128)(2,1)} async-done(((bf16[1152,2,512]{2,1,0:T(2,128)(2,1)}), bf16[1152,2,512]{2,1,0:T(2,128)(2,1)}, u32[]{:S(2)}, u32[]{:S(2)}) %all-to-all-start.1) | async-done | bytes 2359328 | tf_op jit(solution)/shard_map/all_to_all | solution.py:87
  113.6 2.0 %copy.38 = bf16[1152,2,512]{2,0,1:T(8,128)(2,1)S(1)} copy(bf16[1152,2,512]{2,1,0:T(2,128)(2,1)} %all-to-all-done.1) | data formatting | bytes 4718592 | tf_op jit(solution)/shard_map/all_to_all | solution.py:87
  118.0 2.4 %fusion.16 = f32[144,16,512]{2,0,1:T(8,128)S(1)} fusion(f32[144,8,2,512]{3,0,2,1:T(8,128)S(1)} %copy.39, f32[144]{0:T(256)S(1)} %get-tuple-element.22, f32[16,512]{1,0:T(8,128)S(1)} %mul.117, f32[144]{0:T(256)S(1)} %get-tuple-element.21, f32[16,512]{1,0:T(8,128)S(1)} %mul.108, f32[144]{0:T(256)S(1)} %copy-done.8, bf16[144,16,512]{2,1,0:T(8,128)(2,1)S(1)} %copy-done.2), kind=kLoop, calls=%fused_computation.35 | loop fusion | flops 10616832 | bytes 11863744 | tf_op jit(solution)/shard_map/add | solution.py:100
  120.4 2.4 %collective-permute-start.1 = (f32[144,1,512]{2,0,1:T(8,128)S(1)}, f32[144,1,512]{2,0,1:T(8,128)S(1)}, u32[]{:S(2)}, u32[]{:S(2)}) collective-permute-start(f32[144,1,512]{2,0,1:T(8,128)S(1)} %get-tuple-element.13), channel_id=1, source_target_pairs={{1,0},{2,1},{3,2},{5,4},{6,5},{7,6},{9,8},{10,9},{11,10},{13,12},{... | collective-permute-start | bytes 884744 | tf_op jit(solution)/shard_map/ppermute | solution.py:19
  124.0 1.9 fusion.1
  125.9 3.3 %collective-permute-done.1 = f32[144,1,512]{2,0,1:T(8,128)S(1)} collective-permute-done((f32[144,1,512]{2,0,1:T(8,128)S(1)}, f32[144,1,512]{2,0,1:T(8,128)S(1)}, u32[]{:S(2)}, u32[]{:S(2)}) %collective-permute-start.1) | collective-permute-done | bytes 294944 | tf_op jit(solution)/shard_map/ppermute | solution.py:19
  129.2 4.1 %collective-permute-done = f32[144,1,512]{2,0,1:T(8,128)S(1)} collective-permute-done((f32[144,1,512]{2,0,1:T(8,128)S(1)}, f32[144,1,512]{2,0,1:T(8,128)S(1)}, u32[]{:S(2)}, u32[]{:S(2)}) %collective-permute-start) | collective-permute-done | bytes 294944 | tf_op jit(solution)/shard_map/ppermute | solution.py:16
  134.9 2.4 %fusion.27 = f32[144,16,512]{2,0,1:T(8,128)S(1)} fusion(f32[144,17,512]{2,0,1:T(8,128)S(1)} %fusion.12, f32[144,16,512]{2,0,1:T(8,128)S(1)} %fusion.16, f32[144,16,513]{2,0,1:T(8,128)S(1)} %fusion.1, f32[16,512]{1,0:T(8,128)S(1)} %convert_element_type.57), kind=kLoop, calls=%fused_computation.53 | loop fusion | flops 5898240 | bytes 28344320 | tf_op jit(solution)/shard_map/mul | solution.py:61
  137.3 2.4 %collective-permute-start.3 = (f32[144,1,512]{2,0,1:T(8,128)S(1)}, f32[144,1,512]{2,0,1:T(8,128)S(1)}, u32[]{:S(2)}, u32[]{:S(2)}) collective-permute-start(f32[144,1,512]{2,0,1:T(8,128)S(1)} %get-tuple-element.11), channel_id=1, source_target_pairs={{1,0},{2,1},{3,2},{5,4},{6,5},{7,6},{9,8},{10,9},{11,10},{13,12},{... | collective-permute-start | bytes 884744 | tf_op jit(solution)/shard_map/ppermute | solution.py:19
  141.0 3.6 %fusion.4 = f32[144,16,513]{2,0,1:T(8,128)} fusion(f32[144,16,512]{2,0,1:T(8,128)S(1)} %fusion.27, f32[144]{0:T(256)S(1)} %bitcast.54, f32[144]{0:T(256)S(1)} %bitcast.50), kind=kLoop, calls=%fused_computation.14 | loop fusion | flops 3545856 | bytes 9447552 | tf_op jit(solution)/shard_map/add | solution.py:58
  145.0 4.1 %collective-permute-done.2 = f32[144,1,512]{2,0,1:T(8,128)S(1)} collective-permute-done((f32[144,1,512]{2,0,1:T(8,128)S(1)}, f32[144,1,512]{2,0,1:T(8,128)S(1)}, u32[]{:S(2)}, u32[]{:S(2)}) %collective-permute-start.2) | collective-permute-done | bytes 294944 | tf_op jit(solution)/shard_map/ppermute | solution.py:16
  150.7 5.5 %fusion.24 = f32[144,16,512]{2,0,1:T(8,128)S(1)} fusion(f32[144,17,512]{2,0,1:T(8,128)S(1)} %fusion.13, f32[144,16,512]{2,0,1:T(8,128)S(1)} %fusion.27, f32[144,16,513]{2,0,1:T(8,128)} %fusion.4, f32[16,512]{1,0:T(8,128)S(1)} %convert_element_type.57), kind=kLoop, calls=%fused_computation.48 | loop fusion | flops 5898240 | bytes 28344320 | tf_op jit(solution)/shard_map/mul | solution.py:61
  156.3 2.5 %collective-permute-start.5 = (f32[144,1,512]{2,0,1:T(8,128)S(1)}, f32[144,1,512]{2,0,1:T(8,128)S(1)}, u32[]{:S(2)}, u32[]{:S(2)}) collective-permute-start(f32[144,1,512]{2,0,1:T(8,128)S(1)} %get-tuple-element.9), channel_id=1, source_target_pairs={{1,0},{2,1},{3,2},{5,4},{6,5},{7,6},{9,8},{10,9},{11,10},{13,12},{... | collective-permute-start | bytes 884744 | tf_op jit(solution)/shard_map/ppermute | solution.py:19
  160.3 3.6 %fusion.7 = f32[144,16,513]{2,0,1:T(8,128)} fusion(f32[144,16,512]{2,0,1:T(8,128)S(1)} %fusion.24, f32[144]{0:T(256)S(1)} %bitcast.55, f32[144]{0:T(256)S(1)} %bitcast.51), kind=kLoop, calls=%fused_computation.17 | loop fusion | flops 3545856 | bytes 9447552 | tf_op jit(solution)/shard_map/add | solution.py:58
  164.0 3.5 %collective-permute-done.4 = f32[144,1,512]{2,0,1:T(8,128)S(1)} collective-permute-done((f32[144,1,512]{2,0,1:T(8,128)S(1)}, f32[144,1,512]{2,0,1:T(8,128)S(1)}, u32[]{:S(2)}, u32[]{:S(2)}) %collective-permute-start.4) | collective-permute-done | bytes 294944 | tf_op jit(solution)/shard_map/ppermute | solution.py:16
  169.0 5.5 %fusion.21 = f32[144,16,512]{2,0,1:T(8,128)S(1)} fusion(f32[144,17,512]{2,0,1:T(8,128)S(1)} %fusion.14, f32[144,16,512]{2,0,1:T(8,128)S(1)} %fusion.24, f32[144,16,513]{2,0,1:T(8,128)} %fusion.7, f32[16,512]{1,0:T(8,128)S(1)} %convert_element_type.57), kind=kLoop, calls=%fused_computation.43 | loop fusion | flops 5898240 | bytes 28344320 | tf_op jit(solution)/shard_map/mul | solution.py:61
  174.6 2.4 %collective-permute-start.7 = (f32[144,1,512]{2,0,1:T(8,128)S(1)}, f32[144,1,512]{2,0,1:T(8,128)S(1)}, u32[]{:S(2)}, u32[]{:S(2)}) collective-permute-start(f32[144,1,512]{2,0,1:T(8,128)S(1)} %get-tuple-element.7), channel_id=1, source_target_pairs={{1,0},{2,1},{3,2},{5,4},{6,5},{7,6},{9,8},{10,9},{11,10},{13,12},{... | collective-permute-start | bytes 884744 | tf_op jit(solution)/shard_map/ppermute | solution.py:19
  178.3 1.9 fusion.10
  181.2 4.4 %collective-permute-done.6 = f32[144,1,512]{2,0,1:T(8,128)S(1)} collective-permute-done((f32[144,1,512]{2,0,1:T(8,128)S(1)}, f32[144,1,512]{2,0,1:T(8,128)S(1)}, u32[]{:S(2)}, u32[]{:S(2)}) %collective-permute-start.6) | collective-permute-done | bytes 294944 | tf_op jit(solution)/shard_map/ppermute | solution.py:16
  187.2 2.5 %fusion.18 = f32[144,16,512]{2,0,1:T(8,128)S(1)} fusion(f32[144,17,512]{2,0,1:T(8,128)S(1)} %fusion.15, f32[144,16,512]{2,0,1:T(8,128)S(1)} %fusion.21, f32[144,16,513]{2,0,1:T(8,128)S(1)} %fusion.10, f32[16,512]{1,0:T(8,128)S(1)} %convert_element_type.57), kind=kLoop, calls=%fused_computation.38 | loop fusion | flops 5898240 | bytes 28344320 | tf_op jit(solution)/shard_map/mul | solution.py:61
  189.6 4.9 %copy.40 = f32[144,16,512]{2,1,0:T(8,128)} copy(f32[144,16,512]{2,0,1:T(8,128)S(1)} %fusion.18) | data formatting | bytes 9437184 | tf_op jit(solution)/shard_map/mul | solution.py:61
  (58 shorter events, 16.2 us)
Async XLA Ops:
  0.0 60.7 %copy-start = (bf16[1152,1152]{1,0:T(8,128)(2,1)S(1)}, bf16[1152,1152]{1,0:T(8,128)(2,1)}, u32[]{:S(2)}) copy-start(bf16[1152,1152]{1,0:T(8,128)(2,1)} %param.18) | copy-start | bytes 7962628
  0.0 9.3 %copy-start.3 = (s32[1152]{0:T(1024)S(1)}, s32[1152]{0:T(1024)}, u32[]{:S(2)}) copy-start(s32[1152]{0:T(1024)} %param.19) | copy-start | bytes 13828
  4.5 32.9 %all-to-all-start = ((bf16[144,16,512]{2,0,1:T(8,128)(2,1)}), bf16[144,16,512]{2,0,1:T(8,128)(2,1)}, u32[]{:S(2)}, u32[]{:S(2)}) async-start(bf16[144,16,512]{2,0,1:T(8,128)(2,1)} %copy.33), calls=%async_computation | async-start | bytes 4718592 | tf_op jit(solution)/shard_map/all_to_all | solution.py:89
  52.1 8.6 %copy-start.11 = (f32[1152]{0:T(1024)S(1)}, f32[1152]{0:T(1024)}, u32[]{:S(2)}) copy-start(f32[1152]{0:T(1024)} %param.16) | copy-start | bytes 13828
  72.9 12.6 %copy-start.4 = (s32[16,512]{1,0:T(8,128)S(1)}, s32[16,512]{1,0:T(8,128)}, u32[]{:S(2)}) copy-start(s32[16,512]{1,0:T(8,128)} %param.23) | copy-start | bytes 98308
  72.9 12.7 %copy-start.10 = (f32[8,2]{0,1:T(2,128)S(1)}, f32[8,2]{0,1:T(2,128)}, u32[]{:S(2)}) copy-start(f32[8,2]{0,1:T(2,128)} %param.20) | copy-start | bytes 196
  72.9 12.7 %copy-start.6 = (s32[8,32]{1,0:T(8,128)S(1)}, s32[8,32]{1,0:T(8,128)}, u32[]{:S(2)}) copy-start(s32[8,32]{1,0:T(8,128)} %param.21) | copy-start | bytes 3076
  72.9 12.8 %copy-start.5 = (s32[8,32]{1,0:T(8,128)S(1)}, s32[8,32]{1,0:T(8,128)}, u32[]{:S(2)}) copy-start(s32[8,32]{1,0:T(8,128)} %param.22) | copy-start | bytes 3076
  72.9 13.4 %copy-start.9 = (f32[144]{0:T(256)S(1)}, f32[144]{0:T(256)}, u32[]{:S(2)}) copy-start(f32[144]{0:T(256)} %param.13) | copy-start | bytes 1732
  72.9 13.4 %copy-start.7 = (f32[144,2]{0,1:T(2,128)S(1)}, f32[144,2]{0,1:T(2,128)}, u32[]{:S(2)}) copy-start(f32[144,2]{0,1:T(2,128)} %param.15) | copy-start | bytes 3460
  79.7 33.9 %all-to-all-start.1 = ((bf16[1152,2,512]{2,1,0:T(2,128)(2,1)}), bf16[1152,2,512]{2,1,0:T(2,128)(2,1)}, u32[]{:S(2)}, u32[]{:S(2)}) async-start(bf16[1152,2,512]{2,1,0:T(2,128)(2,1)} %copy.37), calls=%async_computation.1 | async-start | bytes 4718592 | tf_op jit(solution)/shard_map/all_to_all | solution.py:87
  116.3 1.7 copy-start.2
  116.3 1.7 copy-start.8
  120.4 8.8 %collective-permute-start.1 = (f32[144,1,512]{2,0,1:T(8,128)S(1)}, f32[144,1,512]{2,0,1:T(8,128)S(1)}, u32[]{:S(2)}, u32[]{:S(2)}) collective-permute-start(f32[144,1,512]{2,0,1:T(8,128)S(1)} %get-tuple-element.13), channel_id=1, source_target_pairs={{1,0},{2,1},{3,2},{5,4},{6,5},{7,6},{9,8},{10,9},{11,10},{13,12},{... | collective-permute-start | bytes 884744 | tf_op jit(solution)/shard_map/ppermute | solution.py:19
  122.7 10.6 %collective-permute-start = (f32[144,1,512]{2,0,1:T(8,128)S(1)}, f32[144,1,512]{2,0,1:T(8,128)S(1)}, u32[]{:S(2)}, u32[]{:S(2)}) collective-permute-start(f32[144,1,512]{2,0,1:T(8,128)S(1)} %get-tuple-element.14), channel_id=1, source_target_pairs={{0,1},{1,2},{2,3},{4,5},{5,6},{6,7},{8,9},{9,10},{10,11},{12,13},{... | collective-permute-start | bytes 884744 | tf_op jit(solution)/shard_map/ppermute | solution.py:16
  137.3 7.7 %collective-permute-start.3 = (f32[144,1,512]{2,0,1:T(8,128)S(1)}, f32[144,1,512]{2,0,1:T(8,128)S(1)}, u32[]{:S(2)}, u32[]{:S(2)}) collective-permute-start(f32[144,1,512]{2,0,1:T(8,128)S(1)} %get-tuple-element.11), channel_id=1, source_target_pairs={{1,0},{2,1},{3,2},{5,4},{6,5},{7,6},{9,8},{10,9},{11,10},{13,12},{... | collective-permute-start | bytes 884744 | tf_op jit(solution)/shard_map/ppermute | solution.py:19
  139.7 9.4 %collective-permute-start.2 = (f32[144,1,512]{2,0,1:T(8,128)S(1)}, f32[144,1,512]{2,0,1:T(8,128)S(1)}, u32[]{:S(2)}, u32[]{:S(2)}) collective-permute-start(f32[144,1,512]{2,0,1:T(8,128)S(1)} %get-tuple-element.12), channel_id=1, source_target_pairs={{0,1},{1,2},{2,3},{4,5},{5,6},{6,7},{8,9},{9,10},{10,11},{12,13},{... | collective-permute-start | bytes 884744 | tf_op jit(solution)/shard_map/ppermute | solution.py:16
  156.3 7.7 %collective-permute-start.5 = (f32[144,1,512]{2,0,1:T(8,128)S(1)}, f32[144,1,512]{2,0,1:T(8,128)S(1)}, u32[]{:S(2)}, u32[]{:S(2)}) collective-permute-start(f32[144,1,512]{2,0,1:T(8,128)S(1)} %get-tuple-element.9), channel_id=1, source_target_pairs={{1,0},{2,1},{3,2},{5,4},{6,5},{7,6},{9,8},{10,9},{11,10},{13,12},{... | collective-permute-start | bytes 884744 | tf_op jit(solution)/shard_map/ppermute | solution.py:19
  158.8 8.6 %collective-permute-start.4 = (f32[144,1,512]{2,0,1:T(8,128)S(1)}, f32[144,1,512]{2,0,1:T(8,128)S(1)}, u32[]{:S(2)}, u32[]{:S(2)}) collective-permute-start(f32[144,1,512]{2,0,1:T(8,128)S(1)} %get-tuple-element.10), channel_id=1, source_target_pairs={{0,1},{1,2},{2,3},{4,5},{5,6},{6,7},{8,9},{9,10},{10,11},{12,13},{... | collective-permute-start | bytes 884744 | tf_op jit(solution)/shard_map/ppermute | solution.py:16
  174.6 6.6 %collective-permute-start.7 = (f32[144,1,512]{2,0,1:T(8,128)S(1)}, f32[144,1,512]{2,0,1:T(8,128)S(1)}, u32[]{:S(2)}, u32[]{:S(2)}) collective-permute-start(f32[144,1,512]{2,0,1:T(8,128)S(1)} %get-tuple-element.7), channel_id=1, source_target_pairs={{1,0},{2,1},{3,2},{5,4},{6,5},{7,6},{9,8},{10,9},{11,10},{13,12},{... | collective-permute-start | bytes 884744 | tf_op jit(solution)/shard_map/ppermute | solution.py:19
  177.0 8.6 %collective-permute-start.6 = (f32[144,1,512]{2,0,1:T(8,128)S(1)}, f32[144,1,512]{2,0,1:T(8,128)S(1)}, u32[]{:S(2)}, u32[]{:S(2)}) collective-permute-start(f32[144,1,512]{2,0,1:T(8,128)S(1)} %get-tuple-element.8), channel_id=1, source_target_pairs={{0,1},{1,2},{2,3},{4,5},{5,6},{6,7},{8,9},{9,10},{10,11},{12,13},{... | collective-permute-start | bytes 884744 | tf_op jit(solution)/shard_map/ppermute | solution.py:16
  187.2 7.4 %copy-start.1 = (bf16[1152,1152]{1,0:T(8,128)(2,1)S(1)}, bf16[1152,1152]{1,0:T(8,128)(2,1)}, u32[]{:S(2)}) copy-start(bf16[1152,1152]{1,0:T(8,128)(2,1)} %param.18) | copy-start | bytes 7962628
where the time goes:
time: 195 us
  waiting for transfers between devices  76 us (39%)
  other arithmetic  40.5 us (21%)
  local copies, waits for them, and re-layouts  39.9 us (20%)
  starting transfers between devices  25.6 us (13%)
  matrix products  12.2 us (6%)
    all_to_all x1, waiting for transfers between devices, per_device(): lax.all_to_all(energy, 'comp', split_axis=1, concat_axis=0, tiled=True)  28 us
    all_to_all x1, waiting for transfers between devices, per_device(): lax.all_to_all(cell_terms(lax.all_to_all(energy, 'comp', split_axis=1, co...  27.2 us
    ppermute x4, waiting for transfers between devices, with_halo(): lax.ppermute(lax.slice_in_dim(block, block.shape[dim] - width, None, axis...  16.1 us
    mul x4, other arithmetic, advect(): (center - (flux_x[..., 1:] - flux_x[..., :-1]) - (flux_y[..., 1:, :] - fl...  15.9 us
    dot_general x1, matrix products, cell_terms(): nonlinear = jnp.dot(transfer, product, preferred_element_type=jnp.float32)  12.2 us
    add x4, other arithmetic, advect(): jnp.maximum(courant_x, 0.0) * padded_x[..., :-1]  11 us
    ppermute x4, starting transfers between devices, with_halo(): lax.ppermute(lax.slice_in_dim(block, 0, width, axis=dim), axis, backward)  9.67 us
    gather x1, local copies, waits for them, and re-layouts, cell_terms(): partner = jnp.take(flattened, pattern, axis=0)  8.59 us
  transfers between devices with their start and end apart: 10, of which 9 were waited for; matrix products, arithmetic and copies ran while one was open for 6% of the time, Pallas kernels for 0%

commit v1 on v0

--- a/solution.py
+++ b/solution.py
@@ -86,7 +86,12 @@
     input_term = growth[:, None, None] * jnp.maximum(0.0, drive) * widened
     returned = lax.all_to_all(
         cell_terms(
-            lax.all_to_all(energy, "comp", split_axis=1, concat_axis=0, tiled=True),
+            jnp.concatenate(
+                lax.all_to_all(
+                    jnp.stack(jnp.split(energy, lax.axis_size("comp"), axis=1)), "comp", 0, 0
+                ),
+                axis=0,
+            ),
             mixing,
             transfer,
             pattern,

time: 195 us -> 210 us (1.077)
  local copies, waits for them, and re-layouts: 39.9 us -> 55.4 us
    unnamed x27 -> x33, local copies, waits for them, and re-layouts: 7.76 us -> 20.8 us
    another operation x0 -> x2, local copies, waits for them, and re-layouts: none -> 6.6 us  [the longest x1 4.31 us: cell_terms(): flattened = spectra.reshape(spectrum_shape[0], -1)]
    gather x1 -> x2, local copies, waits for them, and re-layouts: 8.59 us -> 13 us  [cell_terms(): partner = jnp.take(flattened, pattern, axis=0)]
    reshape x1 -> x0, local copies, waits for them, and re-layouts: 4.37 us -> none  [cell_terms(): flattened = spectra.reshape(spectrum_shape[0], -1)]
    all_to_all x2 -> x1, local copies, waits for them, and re-layouts: 6.13 us -> 2.04 us  [per_device(): lax.all_to_all(cell_terms(jnp.concatenate(lax.all_to_all(jnp.stack(jnp.sp...]
where the time goes in v1:
time: 210 us; the launch traced here: 209 us
  waiting for transfers between devices  76 us (36%)
  local copies, waits for them, and re-layouts  55.4 us (26%)
  other arithmetic  39.9 us (19%)
  starting transfers between devices  25.6 us (12%)
  matrix products  11.3 us (5%)
    all_to_all x1, waiting for transfers between devices, per_device(): lax.all_to_all(jnp.stack(jnp.split(energy, lax.axis_size('comp'), axis=1)...  28 us
    all_to_all x1, waiting for transfers between devices, per_device(): lax.all_to_all(cell_terms(jnp.concatenate(lax.all_to_all(jnp.stack(jnp.sp...  27.2 us
    unnamed x33, local copies, waits for them, and re-layouts  20.8 us
    ppermute x4, waiting for transfers between devices, with_halo(): lax.ppermute(lax.slice_in_dim(block, block.shape[dim] - width, None, axis...  16.1 us
    mul x4, other arithmetic, advect(): (center - (flux_x[..., 1:] - flux_x[..., :-1]) - (flux_y[..., 1:, :] - fl...  15.9 us
    gather x2, local copies, waits for them, and re-layouts, cell_terms(): partner = jnp.take(flattened, pattern, axis=0)  13 us
    dot_general x1, matrix products, cell_terms(): nonlinear = jnp.dot(transfer, product, preferred_element_type=jnp.float32)  11.3 us
    add x4, other arithmetic, advect(): jnp.maximum(courant_x, 0.0) * padded_x[..., :-1]  11 us
  transfers between devices with their start and end apart: 10, of which 9 were waited for; matrix products, arithmetic and copies ran while one was open for 6% of the time, Pallas kernels for 0%

profile of v1, /device:TPU:26, one launch (start us, length us, event | category | flops | bytes accessed | tf_op | source)
XLA Modules:
  0.0 208.7 jit_solution(8088299828358412936)
XLA Ops:
  0.0 2.3 %bitcast_dynamic-update-slice_fusion.7 = bf16[8,144,2,512]{3,2,1,0:T(2,128)(2,1)} fusion(bf16[144,16,512]{2,1,0:T(8,128)(2,1)} %param.12), kind=kLoop, calls=%fused_computation.68 | loop fusion | bytes 589824
  2.3 2.3 %bitcast_dynamic-update-slice_fusion.6 = bf16[8,144,2,512]{3,2,1,0:T(2,128)(2,1)} fusion(bf16[8,144,2,512]{3,2,1,0:T(2,128)(2,1)} %bitcast_dynamic-update-slice_fusion.7, bf16[144,16,512]{2,1,0:T(8,128)(2,1)} %param.12), kind=kLoop, calls=%fused_computation.67 | loop fusion | bytes 589824
  4.6 2.3 %bitcast_dynamic-update-slice_fusion.5 = bf16[8,144,2,512]{3,2,1,0:T(2,128)(2,1)} fusion(bf16[8,144,2,512]{3,2,1,0:T(2,128)(2,1)} %bitcast_dynamic-update-slice_fusion.6, bf16[144,16,512]{2,1,0:T(8,128)(2,1)} %param.12), kind=kLoop, calls=%fused_computation.66 | loop fusion | bytes 589824
  13.6 2.3 %bitcast_dynamic-update-slice_fusion.1 = bf16[8,144,2,512]{3,2,1,0:T(2,128)(2,1)} fusion(bf16[8,144,2,512]{3,2,1,0:T(2,128)(2,1)} %bitcast_dynamic-update-slice_fusion.2, bf16[144,16,512]{2,1,0:T(8,128)(2,1)} %param.12), kind=kLoop, calls=%fused_computation.62 | loop fusion | bytes 589824
  18.2 4.8 %all-to-all-start = ((bf16[8,144,2,512]{3,2,1,0:T(2,128)(2,1)}), bf16[8,144,2,512]{3,2,1,0:T(2,128)(2,1)}, u32[]{:S(2)}, u32[]{:S(2)}) async-start(bf16[8,144,2,512]{3,2,1,0:T(2,128)(2,1)} %bitcast_dynamic-update-slice_fusion), calls=%async_computation | async-start | bytes 4718592 | tf_op jit(solution)/shard_map/all_to_all | solution.py:90
  23.0 28.0 %all-to-all-done = bf16[8,144,2,512]{3,2,1,0:T(2,128)(2,1)} async-done(((bf16[8,144,2,512]{3,2,1,0:T(2,128)(2,1)}), bf16[8,144,2,512]{3,2,1,0:T(2,128)(2,1)}, u32[]{:S(2)}, u32[]{:S(2)}) %all-to-all-start) | async-done | bytes 2359328 | tf_op jit(solution)/shard_map/all_to_all | solution.py:90
  51.0 3.7 %convert_reduce_fusion = f32[2,512]{1,0:T(2,128)S(1)} fusion(bf16[8,144,2,512]{3,2,1,0:T(2,128)(2,1)} %all-to-all-done), kind=kLoop, calls=%fused_computation.60 | loop fusion | flops 2358272 | bytes 2363392 | tf_op jit(solution)/shard_map/reduce_sum | solution.py:44
  54.7 3.7 %copy.38 = bf16[144,8,2,512]{3,1,2,0:T(8,128)(2,1)} copy(bf16[144,8,2,512]{3,2,1,0:T(2,128)(2,1)} %bitcast.24) | data formatting | bytes 4718592
  58.4 4.3 %copy.33 = bf16[1152,1024]{0,1:T(8,128)(2,1)} copy(bf16[1152,1024]{1,0:T(8,128)(2,1)} %bitcast.52) | data formatting | bytes 4718592 | tf_op jit(solution)/shard_map/reshape;reshape | solution.py:38
  62.7 8.6 %gather_fusion = bf16[1152,1024]{1,0:T(8,128)(2,1)} fusion(bf16[1152,1024]{1,0:T(8,128)(2,1)} %bitcast.53, s32[2048]{0:T(1024)S(1)} %pad_clamp_fusion), kind=kCustom, calls=%fused_computation | custom fusion | bytes 4723200 | tf_op jit(solution)/shard_map/jit(_take)/gather | solution.py:40
  71.3 4.4 %copy.32 = bf16[1152,1024]{0,1:T(8,128)(2,1)} copy(bf16[1152,1024]{1,0:T(8,128)(2,1)} %gather_fusion) | data formatting | bytes 4718592 | tf_op jit(solution)/shard_map/jit(_take)/gather | solution.py:40
  75.7 11.3 %fusion.29 = bf16[1152,1024]{0,1:T(8,128)(2,1)} fusion(bf16[1152,1024]{0,1:T(8,128)(2,1)} %copy.33, bf16[1152,1152]{1,0:T(8,128)(2,1)S(1)} %copy-done, f32[1024]{0:T(1024)S(1)} %bitcast.75, f32[1152]{0:T(1024)S(1)} %copy-done.11, bf16[1152,1024]{1,0:T(8,128)(2,1)} %bitcast.54, bf16[1152,1152]{1,0:T(8,128)(2,1)} %param.17, bf16[1152,1024]{0,1:T(8,128)(2,1)} %copy.32, ...), kind=kOutput, calls=%fused_computation.57 | convolution fusion | flops 5446434816 | bytes 14755456 | tf_op jit(solution)/shard_map/dot_general | solution.py:42
  87.1 6.8 %copy.34 = bf16[1152,2,512]{2,1,0:T(2,128)(2,1)} copy(bf16[1152,2,512]{0,2,1:T(8,128)(2,1)} %bitcast.56) | data formatting | bytes 4718592 | tf_op jit(solution)/shard_map/reshape | solution.py:46
  93.9 5.8 %all-to-all-start.1 = ((bf16[1152,2,512]{2,1,0:T(2,128)(2,1)}), bf16[1152,2,512]{2,1,0:T(2,128)(2,1)}, u32[]{:S(2)}, u32[]{:S(2)}) async-start(bf16[1152,2,512]{2,1,0:T(2,128)(2,1)} %copy.34), calls=%async_computation.1 | async-start | bytes 4718592 | tf_op jit(solution)/shard_map/all_to_all | solution.py:87
  100.5 27.2 %all-to-all-done.1 = bf16[1152,2,512]{2,1,0:T(2,128)(2,1)} async-done(((bf16[1152,2,512]{2,1,0:T(2,128)(2,1)}), bf16[1152,2,512]{2,1,0:T(2,128)(2,1)}, u32[]{:S(2)}, u32[]{:S(2)}) %all-to-all-start.1) | async-done | bytes 2359328 | tf_op jit(solution)/shard_map/all_to_all | solution.py:87
  132.1 2.4 %fusion.16 = f32[144,16,512]{2,0,1:T(8,128)S(1)} fusion(f32[144,8,2,512]{3,0,2,1:T(8,128)S(1)} %copy.36, bf16[144,16,512]{2,1,0:T(8,128)(2,1)S(1)} %copy-done.2, f32[144]{0:T(256)S(1)} %get-tuple-element.22, f32[16,512]{1,0:T(8,128)S(1)} %mul.117, f32[144]{0:T(256)S(1)} %get-tuple-element.21, f32[16,512]{1,0:T(8,128)S(1)} %mul.108, f32[144]{0:T(256)S(1)} %copy-done.8), kind=kLoop, calls=%fused_computation.34 | loop fusion | flops 10616832 | bytes 11863744 | tf_op jit(solution)/shard_map/add | solution.py:105
  134.5 2.4 %collective-permute-start.1 = (f32[144,1,512]{2,0,1:T(8,128)S(1)}, f32[144,1,512]{2,0,1:T(8,128)S(1)}, u32[]{:S(2)}, u32[]{:S(2)}) collective-permute-start(f32[144,1,512]{2,0,1:T(8,128)S(1)} %get-tuple-element.13), channel_id=1, source_target_pairs={{1,0},{2,1},{3,2},{5,4},{6,5},{7,6},{9,8},{10,9},{11,10},{13,12},{... | collective-permute-start | bytes 884744 | tf_op jit(solution)/shard_map/ppermute | solution.py:19
  140.1 3.3 %collective-permute-done.1 = f32[144,1,512]{2,0,1:T(8,128)S(1)} collective-permute-done((f32[144,1,512]{2,0,1:T(8,128)S(1)}, f32[144,1,512]{2,0,1:T(8,128)S(1)}, u32[]{:S(2)}, u32[]{:S(2)}) %collective-permute-start.1) | collective-permute-done | bytes 294944 | tf_op jit(solution)/shard_map/ppermute | solution.py:19
  143.4 4.1 %collective-permute-done = f32[144,1,512]{2,0,1:T(8,128)S(1)} collective-permute-done((f32[144,1,512]{2,0,1:T(8,128)S(1)}, f32[144,1,512]{2,0,1:T(8,128)S(1)}, u32[]{:S(2)}, u32[]{:S(2)}) %collective-permute-start) | collective-permute-done | bytes 294944 | tf_op jit(solution)/shard_map/ppermute | solution.py:16
  149.0 2.4 %fusion.27 = f32[144,16,512]{2,0,1:T(8,128)S(1)} fusion(f32[144,17,512]{2,0,1:T(8,128)S(1)} %fusion.12, f32[144,16,512]{2,0,1:T(8,128)S(1)} %fusion.16, f32[144,16,513]{2,0,1:T(8,128)S(1)} %fusion.1, f32[16,512]{1,0:T(8,128)S(1)} %convert_element_type.57), kind=kLoop, calls=%fused_computation.52 | loop fusion | flops 5898240 | bytes 28344320 | tf_op jit(solution)/shard_map/mul | solution.py:61
  151.5 2.4 %collective-permute-start.3 = (f32[144,1,512]{2,0,1:T(8,128)S(1)}, f32[144,1,512]{2,0,1:T(8,128)S(1)}, u32[]{:S(2)}, u32[]{:S(2)}) collective-permute-start(f32[144,1,512]{2,0,1:T(8,128)S(1)} %get-tuple-element.11), channel_id=1, source_target_pairs={{1,0},{2,1},{3,2},{5,4},{6,5},{7,6},{9,8},{10,9},{11,10},{13,12},{... | collective-permute-start | bytes 884744 | tf_op jit(solution)/shard_map/ppermute | solution.py:19
  155.2 3.6 %fusion.4 = f32[144,16,513]{2,0,1:T(8,128)} fusion(f32[144,16,512]{2,0,1:T(8,128)S(1)} %fusion.27, f32[144]{0:T(256)S(1)} %bitcast.72, f32[144]{0:T(256)S(1)} %bitcast.68), kind=kLoop, calls=%fused_computation.14 | loop fusion | flops 3545856 | bytes 9447552 | tf_op jit(solution)/shard_map/add | solution.py:58
  159.2 4.1 %collective-permute-done.2 = f32[144,1,512]{2,0,1:T(8,128)S(1)} collective-permute-done((f32[144,1,512]{2,0,1:T(8,128)S(1)}, f32[144,1,512]{2,0,1:T(8,128)S(1)}, u32[]{:S(2)}, u32[]{:S(2)}) %collective-permute-start.2) | collective-permute-done | bytes 294944 | tf_op jit(solution)/shard_map/ppermute | solution.py:16
  164.9 5.5 %fusion.24 = f32[144,16,512]{2,0,1:T(8,128)S(1)} fusion(f32[144,17,512]{2,0,1:T(8,128)S(1)} %fusion.13, f32[144,16,512]{2,0,1:T(8,128)S(1)} %fusion.27, f32[144,16,513]{2,0,1:T(8,128)} %fusion.4, f32[16,512]{1,0:T(8,128)S(1)} %convert_element_type.57), kind=kLoop, calls=%fused_computation.47 | loop fusion | flops 5898240 | bytes 28344320 | tf_op jit(solution)/shard_map/mul | solution.py:61
  170.4 2.5 %collective-permute-start.5 = (f32[144,1,512]{2,0,1:T(8,128)S(1)}, f32[144,1,512]{2,0,1:T(8,128)S(1)}, u32[]{:S(2)}, u32[]{:S(2)}) collective-permute-start(f32[144,1,512]{2,0,1:T(8,128)S(1)} %get-tuple-element.9), channel_id=1, source_target_pairs={{1,0},{2,1},{3,2},{5,4},{6,5},{7,6},{9,8},{10,9},{11,10},{13,12},{... | collective-permute-start | bytes 884744 | tf_op jit(solution)/shard_map/ppermute | solution.py:19
  174.5 3.6 %fusion.7 = f32[144,16,513]{2,0,1:T(8,128)} fusion(f32[144,16,512]{2,0,1:T(8,128)S(1)} %fusion.24, f32[144]{0:T(256)S(1)} %bitcast.73, f32[144]{0:T(256)S(1)} %bitcast.69), kind=kLoop, calls=%fused_computation.17 | loop fusion | flops 3545856 | bytes 9447552 | tf_op jit(solution)/shard_map/add | solution.py:58
  178.1 3.5 %collective-permute-done.4 = f32[144,1,512]{2,0,1:T(8,128)S(1)} collective-permute-done((f32[144,1,512]{2,0,1:T(8,128)S(1)}, f32[144,1,512]{2,0,1:T(8,128)S(1)}, u32[]{:S(2)}, u32[]{:S(2)}) %collective-permute-start.4) | collective-permute-done | bytes 294944 | tf_op jit(solution)/shard_map/ppermute | solution.py:16
  183.1 5.5 %fusion.21 = f32[144,16,512]{2,0,1:T(8,128)S(1)} fusion(f32[144,17,512]{2,0,1:T(8,128)S(1)} %fusion.14, f32[144,16,512]{2,0,1:T(8,128)S(1)} %fusion.24, f32[144,16,513]{2,0,1:T(8,128)} %fusion.7, f32[16,512]{1,0:T(8,128)S(1)} %convert_element_type.57), kind=kLoop, calls=%fused_computation.42 | loop fusion | flops 5898240 | bytes 28344320 | tf_op jit(solution)/shard_map/mul | solution.py:61
  188.7 2.4 %collective-permute-start.7 = (f32[144,1,512]{2,0,1:T(8,128)S(1)}, f32[144,1,512]{2,0,1:T(8,128)S(1)}, u32[]{:S(2)}, u32[]{:S(2)}) collective-permute-start(f32[144,1,512]{2,0,1:T(8,128)S(1)} %get-tuple-element.7), channel_id=1, source_target_pairs={{1,0},{2,1},{3,2},{5,4},{6,5},{7,6},{9,8},{10,9},{11,10},{13,12},{... | collective-permute-start | bytes 884744 | tf_op jit(solution)/shard_map/ppermute | solution.py:19
  195.4 4.4 %collective-permute-done.6 = f32[144,1,512]{2,0,1:T(8,128)S(1)} collective-permute-done((f32[144,1,512]{2,0,1:T(8,128)S(1)}, f32[144,1,512]{2,0,1:T(8,128)S(1)}, u32[]{:S(2)}, u32[]{:S(2)}) %collective-permute-start.6) | collective-permute-done | bytes 294944 | tf_op jit(solution)/shard_map/ppermute | solution.py:16
  201.3 2.5 %fusion.18 = f32[144,16,512]{2,0,1:T(8,128)S(1)} fusion(f32[144,17,512]{2,0,1:T(8,128)S(1)} %fusion.15, f32[144,16,512]{2,0,1:T(8,128)S(1)} %fusion.21, f32[144,16,513]{2,0,1:T(8,128)S(1)} %fusion.10, f32[16,512]{1,0:T(8,128)S(1)} %convert_element_type.57), kind=kLoop, calls=%fused_computation.37 | loop fusion | flops 5898240 | bytes 28344320 | tf_op jit(solution)/shard_map/mul | solution.py:61
  203.8 4.9 %copy.37 = f32[144,16,512]{2,1,0:T(8,128)} copy(f32[144,16,512]{2,0,1:T(8,128)S(1)} %fusion.18) | data formatting | bytes 9437184 | tf_op jit(solution)/shard_map/mul | solution.py:61
  (65 shorter events, 31.1 us)
Async XLA Ops:
  0.0 75.7 %copy-start = (bf16[1152,1152]{1,0:T(8,128)(2,1)S(1)}, bf16[1152,1152]{1,0:T(8,128)(2,1)}, u32[]{:S(2)}) copy-start(bf16[1152,1152]{1,0:T(8,128)(2,1)} %param.18) | copy-start | bytes 7962628
  0.0 23.0 %copy-start.3 = (s32[1152]{0:T(1024)S(1)}, s32[1152]{0:T(1024)}, u32[]{:S(2)}) copy-start(s32[1152]{0:T(1024)} %param.19) | copy-start | bytes 13828
  18.2 32.9 %all-to-all-start = ((bf16[8,144,2,512]{3,2,1,0:T(2,128)(2,1)}), bf16[8,144,2,512]{3,2,1,0:T(2,128)(2,1)}, u32[]{:S(2)}, u32[]{:S(2)}) async-start(bf16[8,144,2,512]{3,2,1,0:T(2,128)(2,1)} %bitcast_dynamic-update-slice_fusion), calls=%async_computation | async-start | bytes 4718592 | tf_op jit(solution)/shard_map/all_to_all | solution.py:90
  71.3 4.4 %copy-start.11 = (f32[1152]{0:T(1024)S(1)}, f32[1152]{0:T(1024)}, u32[]{:S(2)}) copy-start(f32[1152]{0:T(1024)} %param.16) | copy-start | bytes 13828
  87.0 12.6 %copy-start.4 = (s32[16,512]{1,0:T(8,128)S(1)}, s32[16,512]{1,0:T(8,128)}, u32[]{:S(2)}) copy-start(s32[16,512]{1,0:T(8,128)} %param.23) | copy-start | bytes 98308
  87.0 12.7 %copy-start.10 = (f32[8,2]{0,1:T(2,128)S(1)}, f32[8,2]{0,1:T(2,128)}, u32[]{:S(2)}) copy-start(f32[8,2]{0,1:T(2,128)} %param.20) | copy-start | bytes 196
  87.0 12.7 %copy-start.6 = (s32[8,32]{1,0:T(8,128)S(1)}, s32[8,32]{1,0:T(8,128)}, u32[]{:S(2)}) copy-start(s32[8,32]{1,0:T(8,128)} %param.21) | copy-start | bytes 3076
  87.0 12.8 %copy-start.5 = (s32[8,32]{1,0:T(8,128)S(1)}, s32[8,32]{1,0:T(8,128)}, u32[]{:S(2)}) copy-start(s32[8,32]{1,0:T(8,128)} %param.22) | copy-start | bytes 3076
  87.0 13.4 %copy-start.9 = (f32[144]{0:T(256)S(1)}, f32[144]{0:T(256)}, u32[]{:S(2)}) copy-start(f32[144]{0:T(256)} %param.13) | copy-start | bytes 1732
  87.1 13.4 %copy-start.7 = (f32[144,2]{0,1:T(2,128)S(1)}, f32[144,2]{0,1:T(2,128)}, u32[]{:S(2)}) copy-start(f32[144,2]{0,1:T(2,128)} %param.15) | copy-start | bytes 3460
  93.9 33.8 %all-to-all-start.1 = ((bf16[1152,2,512]{2,1,0:T(2,128)(2,1)}), bf16[1152,2,512]{2,1,0:T(2,128)(2,1)}, u32[]{:S(2)}, u32[]{:S(2)}) async-start(bf16[1152,2,512]{2,1,0:T(2,128)(2,1)} %copy.34), calls=%async_computation.1 | async-start | bytes 4718592 | tf_op jit(solution)/shard_map/all_to_all | solution.py:87
  130.4 1.7 copy-start.2
  130.4 1.7 copy-start.8
  134.5 8.8 %collective-permute-start.1 = (f32[144,1,512]{2,0,1:T(8,128)S(1)}, f32[144,1,512]{2,0,1:T(8,128)S(1)}, u32[]{:S(2)}, u32[]{:S(2)}) collective-permute-start(f32[144,1,512]{2,0,1:T(8,128)S(1)} %get-tuple-element.13), channel_id=1, source_target_pairs={{1,0},{2,1},{3,2},{5,4},{6,5},{7,6},{9,8},{10,9},{11,10},{13,12},{... | collective-permute-start | bytes 884744 | tf_op jit(solution)/shard_map/ppermute | solution.py:19
  136.9 10.6 %collective-permute-start = (f32[144,1,512]{2,0,1:T(8,128)S(1)}, f32[144,1,512]{2,0,1:T(8,128)S(1)}, u32[]{:S(2)}, u32[]{:S(2)}) collective-permute-start(f32[144,1,512]{2,0,1:T(8,128)S(1)} %get-tuple-element.14), channel_id=1, source_target_pairs={{0,1},{1,2},{2,3},{4,5},{5,6},{6,7},{8,9},{9,10},{10,11},{12,13},{... | collective-permute-start | bytes 884744 | tf_op jit(solution)/shard_map/ppermute | solution.py:16
  151.5 7.7 %collective-permute-start.3 = (f32[144,1,512]{2,0,1:T(8,128)S(1)}, f32[144,1,512]{2,0,1:T(8,128)S(1)}, u32[]{:S(2)}, u32[]{:S(2)}) collective-permute-start(f32[144,1,512]{2,0,1:T(8,128)S(1)} %get-tuple-element.11), channel_id=1, source_target_pairs={{1,0},{2,1},{3,2},{5,4},{6,5},{7,6},{9,8},{10,9},{11,10},{13,12},{... | collective-permute-start | bytes 884744 | tf_op jit(solution)/shard_map/ppermute | solution.py:19
  153.9 9.4 %collective-permute-start.2 = (f32[144,1,512]{2,0,1:T(8,128)S(1)}, f32[144,1,512]{2,0,1:T(8,128)S(1)}, u32[]{:S(2)}, u32[]{:S(2)}) collective-permute-start(f32[144,1,512]{2,0,1:T(8,128)S(1)} %get-tuple-element.12), channel_id=1, source_target_pairs={{0,1},{1,2},{2,3},{4,5},{5,6},{6,7},{8,9},{9,10},{10,11},{12,13},{... | collective-permute-start | bytes 884744 | tf_op jit(solution)/shard_map/ppermute | solution.py:16
  170.4 7.7 %collective-permute-start.5 = (f32[144,1,512]{2,0,1:T(8,128)S(1)}, f32[144,1,512]{2,0,1:T(8,128)S(1)}, u32[]{:S(2)}, u32[]{:S(2)}) collective-permute-start(f32[144,1,512]{2,0,1:T(8,128)S(1)} %get-tuple-element.9), channel_id=1, source_target_pairs={{1,0},{2,1},{3,2},{5,4},{6,5},{7,6},{9,8},{10,9},{11,10},{13,12},{... | collective-permute-start | bytes 884744 | tf_op jit(solution)/shard_map/ppermute | solution.py:19
  173.0 8.6 %collective-permute-start.4 = (f32[144,1,512]{2,0,1:T(8,128)S(1)}, f32[144,1,512]{2,0,1:T(8,128)S(1)}, u32[]{:S(2)}, u32[]{:S(2)}) collective-permute-start(f32[144,1,512]{2,0,1:T(8,128)S(1)} %get-tuple-element.10), channel_id=1, source_target_pairs={{0,1},{1,2},{2,3},{4,5},{5,6},{6,7},{8,9},{9,10},{10,11},{12,13},{... | collective-permute-start | bytes 884744 | tf_op jit(solution)/shard_map/ppermute | solution.py:16
  188.7 6.6 %collective-permute-start.7 = (f32[144,1,512]{2,0,1:T(8,128)S(1)}, f32[144,1,512]{2,0,1:T(8,128)S(1)}, u32[]{:S(2)}, u32[]{:S(2)}) collective-permute-start(f32[144,1,512]{2,0,1:T(8,128)S(1)} %get-tuple-element.7), channel_id=1, source_target_pairs={{1,0},{2,1},{3,2},{5,4},{6,5},{7,6},{9,8},{10,9},{11,10},{13,12},{... | collective-permute-start | bytes 884744 | tf_op jit(solution)/shard_map/ppermute | solution.py:19
  191.1 8.6 %collective-permute-start.6 = (f32[144,1,512]{2,0,1:T(8,128)S(1)}, f32[144,1,512]{2,0,1:T(8,128)S(1)}, u32[]{:S(2)}, u32[]{:S(2)}) collective-permute-start(f32[144,1,512]{2,0,1:T(8,128)S(1)} %get-tuple-element.8), channel_id=1, source_target_pairs={{0,1},{1,2},{2,3},{4,5},{5,6},{6,7},{8,9},{9,10},{10,11},{12,13},{... | collective-permute-start | bytes 884744 | tf_op jit(solution)/shard_map/ppermute | solution.py:16
  201.3 7.4 %copy-start.1 = (bf16[1152,1152]{1,0:T(8,128)(2,1)S(1)}, bf16[1152,1152]{1,0:T(8,128)(2,1)}, u32[]{:S(2)}) copy-start(bf16[1152,1152]{1,0:T(8,128)(2,1)} %param.18) | copy-start | bytes 7962628
